TPU v7x, 32 devices: a whole 2x2x4 slice. The times are simulated.
32 devices in a mesh: group: 2 (over y), expert: 4 (over z), query: 2 (over x), dp: 2 (over core).
Axes of the slice: x: 2, y: 2, z: 4, core: 2. Of those that a mesh axis runs over, the one named last changes fastest.
Arguments:
- tokens: bfloat16 [4096, 2048], P(('group', 'expert', 'query', 'dp')), parts along dimension 0, may hold values from -6 to 6
- route_ids: int32 [4096, 4], P(('group', 'expert', 'query', 'dp')), parts along dimension 0, may hold values from 0 to 7, all different within a row; in each aligned block of 128 rows (0 to 127, 128 to 255, ...) at most 128 rows name the same one
- gate_values: float32 [4096, 4], P(('group', 'expert', 'query', 'dp')), parts along dimension 0, may hold values from 0.1 to 1
- passage_lengths: int32 [64], P(('group', 'expert', 'query', 'dp')), parts along dimension 0, may hold values from 16 to 64
- gate_weight: bfloat16 [8, 2048, 384], P(('expert', 'query'), None, 'dp'), may hold values from -0.125 to 0.125
- up_weight: bfloat16 [8, 2048, 384], P(('expert', 'query'), None, 'dp'), may hold values from -0.125 to 0.125
- down_weight: bfloat16 [8, 2048, 384], P(('expert', 'query'), None, 'dp'), may hold values from -0.3125 to 0.3125
- proj_weight: bfloat16 [2048, 128], replicated, may hold values from -0.125 to 0.125
- queries: bfloat16 [128, 32, 128], P(('group', 'query')), parts along dimension 0, may hold values from -0.59765625 to 0.59765625
Outputs:
- scores: float32 [64, 64], P(('group', 'expert', 'query', 'dp')), parts along dimension 0
There are 2 independent parts, one for each index of `group`. A program takes and returns all parts, laid end to end along the dimension named above; an argument that names none is the same for every part. Nothing has to cross between parts.
Inputs may be any that keep to these rules, and one draw needn't show every extreme that they name: `route_ids`: in the rows of one device no expert is named more than 128 times, a bound that some block reaches.
All inputs are finite; a program needn't handle non-finite values.
Results may differ from a plain program's by a relative error of at most 0.0006.
Values may be sent and summed in bfloat16 or wider, within the bound.
A program may use at most 64 MiB of HBM per device.

v0:
```python
import jax
import jax.numpy as jnp
from jax import lax
from jax.sharding import PartitionSpec as P

PLEN = 64


def passage_scores(embedding, live_mask, block_queries):
    query_rows = block_queries.reshape(-1, block_queries.shape[-1])
    raw_scores = jnp.dot(embedding, query_rows.T, preferred_element_type=jnp.float32)
    raw_scores = jnp.where(live_mask[:, None], raw_scores, -jnp.inf)
    best_match = jnp.max(raw_scores.reshape(-1, PLEN, raw_scores.shape[-1]), axis=1)
    return jnp.sum(best_match.reshape(best_match.shape[0], -1, block_queries.shape[1]), axis=-1)


def on_device(
    tokens,
    route_ids,
    gate_values,
    passage_lengths,
    gate_weight,
    up_weight,
    down_weight,
    proj_weight,
    queries,
):
    tok_rows, model_width = tokens.shape
    top_count = route_ids.shape[1]
    experts = lax.axis_size("expert") * lax.axis_size("query")
    capacity = max(2, 2 * tok_rows * top_count // experts)
    assignments = tok_rows * top_count
    flat_routes = route_ids.reshape(-1)
    one_hot = (flat_routes[:, None] == jnp.arange(experts, dtype=jnp.int32)[None, :]).astype(
        jnp.int32
    )
    earlier = jnp.cumsum(one_hot, axis=0) - one_hot
    slot_index = jnp.sum(earlier * one_hot, axis=1)
    slot_target = flat_routes * capacity + slot_index
    slot_owner = (
        jnp.full((experts * capacity,), assignments, jnp.int32)
        .at[slot_target]
        .set(jnp.arange(assignments, dtype=jnp.int32))
    )
    padded = jnp.concatenate([tokens, jnp.zeros((1, model_width), tokens.dtype)], axis=0)
    source_row = jnp.where(slot_owner < assignments, slot_owner // top_count, tok_rows)
    outgoing = padded[source_row].reshape(experts, capacity, model_width)
    arrived = lax.all_to_all(outgoing, ("expert", "query"), split_axis=0, concat_axis=0, tiled=True)
    expert_rows = arrived.reshape(experts * capacity, model_width)
    gate_act = jnp.dot(
        expert_rows,
        lax.all_gather(gate_weight[0], "dp", axis=1, tiled=True),
        preferred_element_type=jnp.float32,
    )
    up_act = jnp.dot(
        expert_rows,
        lax.all_gather(up_weight[0], "dp", axis=1, tiled=True),
        preferred_element_type=jnp.float32,
    )
    hidden = (jax.nn.silu(gate_act) * up_act).astype(jnp.bfloat16)
    accumulated = lax.dot_general(
        hidden,
        lax.all_gather(down_weight[0], "dp", axis=1, tiled=True),
        (((1,), (1,)), ((), ())),
        preferred_element_type=jnp.float32,
    )
    results = accumulated.astype(jnp.bfloat16)
    weights = gate_values.reshape(assignments, 1)
    folded = jnp.dot(results, proj_weight, preferred_element_type=jnp.float32)
    returned_rows = lax.all_to_all(
        folded.reshape(experts, capacity, folded.shape[-1]),
        ("expert", "query"),
        split_axis=0,
        concat_axis=0,
        tiled=True,
    )
    picked = returned_rows.reshape(experts * capacity, folded.shape[-1])[slot_target]
    projected = jnp.dot(tokens, proj_weight, preferred_element_type=jnp.float32) + jnp.sum(
        (picked * weights).reshape(tok_rows, top_count, folded.shape[-1]), axis=1
    )
    lengths_norm = jnp.sqrt(jnp.sum(projected * projected, axis=-1, keepdims=True) + 1e-06)
    embedding = (projected / lengths_norm).astype(jnp.bfloat16)
    position = jnp.arange(tok_rows, dtype=jnp.int32) % PLEN
    live_mask = position < jnp.repeat(passage_lengths, PLEN)
    return passage_scores(
        embedding, live_mask, lax.all_gather(queries, "query", axis=0, tiled=True)
    )


def solution(mesh):
    in_specs = (
        P(("group", "expert", "query", "dp"), None),
        P(("group", "expert", "query", "dp"), None),
        P(("group", "expert", "query", "dp"), None),
        P(("group", "expert", "query", "dp")),
        P(("expert", "query"), None, "dp"),
        P(("expert", "query"), None, "dp"),
        P(("expert", "query"), None, "dp"),
        P(),
        P(("group", "query"), None, None),
    )
    out_specs = P(("group", "expert", "query", "dp"), None)
    return jax.shard_map(
        on_device, mesh=mesh, in_specs=in_specs, out_specs=out_specs, check_vma=False
    )
```

profile of v0, /device:TPU:1, one launch (start us, length us, event | category | flops | bytes accessed | tf_op | source)
XLA Modules:
  0.0 161.9 jit_solution(16316723009276893319)
XLA Ops:
  6.5 0.0 copy-start
  6.5 0.8 copy.16
  7.4 0.1 eq.31
  7.5 0.1 eq.27
  7.6 0.7 broadcast_multiply_fusion
  8.3 1.1 reduce-window.6
  9.4 0.2 slice_reduce_fusion
  9.7 0.1 copy.15
  9.8 0.1 mul.40
  9.9 0.1 fusion.14
  10.0 2.4 %scatter_custom_fusion = s32[1024]{0:T(1024)S(1)} fusion(s32[512]{0:T(512)S(1)} %bitcast.41, s32[512]{0:T(512)S(1)} %iota.17, s32[]{:T(128)} %constant.46.clone.1), kind=kCustom, calls=%fused_computation.38 | custom fusion | bytes 4100 | tf_op jit(solution)/shard_map/scatter | solution.py:43
  12.5 1.1 concatenate.3
  13.6 6.0 %gather_fusion = bf16[1024,2048]{1,0:T(8,128)(2,1)} fusion(bf16[129,2048]{1,0:T(8,128)(2,1)S(1)} %concatenate.3, s32[1024]{0:T(1024)S(1)} %fusion.18), kind=kCustom, calls=%fused_computation | custom fusion | bytes 8392704 | tf_op jit(solution)/shard_map/gather | solution.py:47
  19.6 6.3 %all-to-all-start = ((bf16[8,128,2048]{2,1,0:T(8,128)(2,1)}), bf16[8,128,2048]{2,1,0:T(8,128)(2,1)}, u32[]{:S(2)}, u32[]{:S(2)}) async-start(bf16[8,128,2048]{2,1,0:T(8,128)(2,1)} %bitcast.37), calls=%async_computation | async-start | bytes 8388608 | tf_op jit(solution)/shard_map/all_to_all | solution.py:48
  26.0 0.0 all-gather.7.cloned.1.call-start
  26.0 0.7 all-gather.7.cloned.1.call-update
  26.7 0.0 all-gather.9.cloned.1.call-start
  26.7 0.7 all-gather.9.cloned.1.call-update
  27.4 0.0 all-gather.11.cloned.1.call-start
  27.5 0.7 all-gather.11.cloned.1.call-update
  28.2 12.1 %all-gather.7.cloned.1.call-done = bf16[1,2048,384]{1,2,0:T(8,128)(2,1)} async-done(((bf16[1,2048,192]{1,2,0:T(8,128)(2,1)}), bf16[1,2048,384]{1,2,0:T(8,128)(2,1)}) %all-gather.7.cloned.1.call-update) | async-done | bytes 1572880 | tf_op jit(solution)/shard_map/all_gather | solution.py:52
  40.2 78.2 %all-to-all-done = bf16[8,128,2048]{2,1,0:T(8,128)(2,1)} async-done(((bf16[8,128,2048]{2,1,0:T(8,128)(2,1)}), bf16[8,128,2048]{2,1,0:T(8,128)(2,1)}, u32[]{:S(2)}, u32[]{:S(2)}) %all-to-all-start) | async-done | bytes 4194336 | tf_op jit(solution)/shard_map/all_to_all | solution.py:48
  118.4 5.0 %fusion.8 = f32[1024,384]{1,0:T(8,128)S(1)} fusion(bf16[1024,2048]{1,0:T(8,128)(2,1)} %bitcast.5, bf16[1,2048,384]{1,2,0:T(8,128)(2,1)} %all-gather.7.cloned.1.call-done), kind=kOutput, calls=%fused_computation.10 | convolution fusion | flops 1610612736 | bytes 7340032 | tf_op jit(solution)/shard_map/dot_general | solution.py:50
  123.5 0.0 all-gather.9.cloned.1.call-done
  123.5 5.1 %multiply_convert_fusion = bf16[1024,384]{1,0:T(8,128)(2,1)S(1)} fusion(f32[1024,384]{1,0:T(8,128)S(1)} %fusion.8, bf16[1024,2048]{1,0:T(8,128)(2,1)} %bitcast.5, bf16[1,2048,384]{1,2,0:T(8,128)(2,1)} %all-gather.9.cloned.1.call-done), kind=kOutput, calls=%fused_computation.12 | convolution fusion | flops 1612972032 | bytes 8126464 | tf_op jit(solution)/shard_map/dot_general | solution.py:55
  128.6 0.0 copy-start.3
  128.6 0.0 copy-start.4
  128.6 0.0 copy-start.2
  128.6 0.0 all-gather.11.cloned.1.call-done
  128.7 0.0 copy-done
  128.7 5.7 %fusion = f32[1024,128]{1,0:T(8,128)} fusion(bf16[2048,128]{1,0:T(8,128)(2,1)S(1)} %copy-done, bf16[1024,384]{1,0:T(8,128)(2,1)S(1)} %multiply_convert_fusion, bf16[1,2048,384]{1,2,0:T(8,128)(2,1)} %all-gather.11.cloned.1.call-done), kind=kOutput, calls=%fused_computation.3 | convolution fusion | flops 2149580800 | bytes 3407872 | tf_op jit(solution)/shard_map/dot_general | solution.py:69
  134.4 4.6 %all-to-all-start.1 = ((f32[8,128,128]{2,1,0:T(8,128)}), f32[8,128,128]{2,1,0:T(8,128)S(1)}, u32[]{:S(2)}, u32[]{:S(2)}) async-start(f32[8,128,128]{2,1,0:T(8,128)} %bitcast.9), calls=%async_computation.1 | async-start | bytes 1048576 | tf_op jit(solution)/shard_map/all_to_all | solution.py:70
  139.0 0.0 copy-done.3
  139.0 0.1 copy.18
  139.1 0.0 copy-done.4
  139.1 0.1 broadcast_in_dim.28
  139.2 0.1 reshape.99
  139.3 0.0 copy-done.2
  139.3 12.0 %all_gather.15 = bf16[64,32,128]{2,1,0:T(8,128)(2,1)S(1)} all-gather(bf16[32,32,128]{2,1,0:T(8,128)(2,1)S(1)} %copy-done.2), channel_id=1, replica_groups=mesh['group'=2,'expert'=4,'query'=2,'dp'=2] {'query'}, dimensions={0}, use_global_device_ids=true | all-gather | bytes 786432 | tf_op jit(solution)/shard_map/all_gather | solution.py:86
  151.3 0.0 copy-start.1
  151.3 1.2 all-to-all-done.1
  152.5 1.0 gather_fusion.1
  153.6 0.2 multiply_reduce_fusion
  153.8 0.1 copy.19
  153.9 0.0 copy-done.1
  153.9 0.4 multiply_reduce_fusion.1
  154.3 0.4 bitcast_reduce_fusion
  154.6 0.1 reshape.107
  154.8 0.7 reduce_sum.42
  (9 shorter events, 0.1 us)
Async XLA Ops:
  6.5 122.1 %copy-start = (bf16[2048,128]{1,0:T(8,128)(2,1)S(1)}, bf16[2048,128]{1,0:T(8,128)(2,1)}, u32[]{:S(2)}) copy-start(bf16[2048,128]{1,0:T(8,128)(2,1)} %param.16) | copy-start | bytes 1572868
  19.6 98.8 %all-to-all-start = ((bf16[8,128,2048]{2,1,0:T(8,128)(2,1)}), bf16[8,128,2048]{2,1,0:T(8,128)(2,1)}, u32[]{:S(2)}, u32[]{:S(2)}) async-start(bf16[8,128,2048]{2,1,0:T(8,128)(2,1)} %bitcast.37), calls=%async_computation | async-start | bytes 8388608 | tf_op jit(solution)/shard_map/all_to_all | solution.py:48
  26.0 14.3 %all-gather.7.cloned.1.call-start = ((), (), s32[]{:S(2)}) async-start(), calls=%async_computation.2 | async-start | bytes 2359296 | tf_op jit(solution)/shard_map/all_gather | solution.py:52
  26.7 96.8 %all-gather.9.cloned.1.call-start = ((), (), s32[]{:S(2)}) async-start(), calls=%async_computation.3 | async-start | bytes 2359296 | tf_op jit(solution)/shard_map/all_gather | solution.py:57
  27.4 101.2 %all-gather.11.cloned.1.call-start = ((), (), s32[]{:S(2)}) async-start(), calls=%async_computation.4 | async-start | bytes 2359296 | tf_op jit(solution)/shard_map/all_gather | solution.py:63
  128.6 10.4 %copy-start.3 = (f32[128,4]{0,1:T(4,128)S(1)}, f32[128,4]{0,1:T(4,128)}, u32[]{:S(2)}) copy-start(f32[128,4]{0,1:T(4,128)} %param.11) | copy-start | bytes 6148
  128.6 10.5 %copy-start.4 = (s32[2]{0:T(128)S(1)}, s32[2]{0:T(128)}, u32[]{:S(2)}) copy-start(s32[2]{0:T(128)} %param.12) | copy-start | bytes 28
  128.6 10.7 %copy-start.2 = (bf16[32,32,128]{2,1,0:T(8,128)(2,1)S(1)}, bf16[32,32,128]{2,1,0:T(8,128)(2,1)}, u32[]{:S(2)}) copy-start(bf16[32,32,128]{2,1,0:T(8,128)(2,1)} %param.17) | copy-start | bytes 786436
  134.4 18.2 %all-to-all-start.1 = ((f32[8,128,128]{2,1,0:T(8,128)}), f32[8,128,128]{2,1,0:T(8,128)S(1)}, u32[]{:S(2)}, u32[]{:S(2)}) async-start(f32[8,128,128]{2,1,0:T(8,128)} %bitcast.9), calls=%async_computation.1 | async-start | bytes 1048576 | tf_op jit(solution)/shard_map/all_to_all | solution.py:70
  151.3 2.6 %copy-start.1 = (bf16[128,2048]{1,0:T(8,128)(2,1)S(1)}, bf16[128,2048]{1,0:T(8,128)(2,1)}, u32[]{:S(2)}) copy-start(bf16[128,2048]{1,0:T(8,128)(2,1)} %param.9) | copy-start | bytes 1572868
Sparse Core Ops, SparseCore 0:
  28.3 11.8 all-gather.6
  41.8 10.9 all-gather.8
  54.3 10.9 all-gather.10
where the time goes:
time: 164 us; the launch traced here: 162 us
  waiting for transfers between devices  93.6 us (57%)
  matrix products  16.6 us (10%)
  between operations  13.3 us (8%)
  local copies, waits for them, and re-layouts  12.6 us (8%)
  blocking collectives  12 us (7%)
  starting transfers between devices  11.1 us (7%)
  other arithmetic  2.88 us (2%)
    all_to_all x1, waiting for transfers between devices, on_device(): lax.all_to_all(outgoing, ('expert', 'query'), split_axis=0, concat_axis=0...  78.2 us
    all_gather x1, waiting for transfers between devices, on_device(): lax.all_gather(gate_weight[0], 'dp', axis=1, tiled=True)  12.1 us
    all_gather x1, blocking collectives, on_device(): lax.all_gather(queries, 'query', axis=0, tiled=True)  12 us
    all_to_all x1, starting transfers between devices, on_device(): lax.all_to_all(outgoing, ('expert', 'query'), split_axis=0, concat_axis=0...  6.34 us
    gather x1, local copies, waits for them, and re-layouts, on_device(): outgoing = padded[source_row].reshape(experts, capacity, model_width)  6.03 us
    dot_general x1, matrix products, on_device(): folded = jnp.dot(results, proj_weight, preferred_element_type=jnp.float32)  5.7 us
    dot_general x1, matrix products, on_device(): jnp.dot(expert_rows, lax.all_gather(up_weight[0], 'dp', axis=1, tiled=Tru...  5.12 us
    dot_general x1, matrix products, on_device(): jnp.dot(expert_rows, lax.all_gather(gate_weight[0], 'dp', axis=1, tiled=T...  5.02 us
  transfers between devices with their start and end apart: 5, of which 3 were waited for; matrix products, arithmetic and copies ran while one was open for 6% of the time, Pallas kernels for 0%

commit v1 on v0

--- a/solution.py
+++ b/solution.py
@@ -1,9 +1,483 @@
+import functools
+
 import jax
 import jax.numpy as jnp
 from jax import lax
+from jax.experimental import pallas as pl
+from jax.experimental.pallas import tpu as pltpu
 from jax.sharding import PartitionSpec as P
 
 PLEN = 64
+MESH = pl.DeviceIdType.MESH
+LANES = 128
+PIECES = 2
+W_PIECES = 2
+
+
+def when_all(conds, body):
+    live = [c for c in conds if c is not None]
+    if live:
+        pl.when(functools.reduce(jnp.logical_and, live))(body)
+    else:
+        body()
+
+
+def dense_kernel(
+    n_exp,
+    tokens,
+    gate,
+    up,
+    down,
+    proj,
+    queries,
+    routes,
+    gates,
+    plens,
+    out,
+    tok,
+    gate_v,
+    up_v,
+    down_v,
+    proj_v,
+    w_all,
+    v_all,
+    q_all,
+    comb,
+    acc,
+    ret,
+    base,
+    local_sem,
+    tok_ss,
+    tok_rs,
+    comb_ss,
+    comb_rs,
+    own_ss,
+    own_rs,
+    wx_ss,
+    wx_rs,
+    wy_ss,
+    wy_rs,
+    wd_ss,
+    wd_rs,
+    v_ss,
+    v_rs,
+    q_ss,
+    q_rs,
+    ret_ss,
+    ret_rs,
+):
+    z, x = lax.axis_index("expert"), lax.axis_index("query")
+    y, c = lax.axis_index("group"), lax.axis_index("dp")
+    rows, width = tokens.shape
+    units = gate.shape[1]
+    full = units // LANES * LANES
+    piece = rows // PIECES
+    half_rows = width // 2
+    w_rows = half_rows // W_PIECES
+    top = routes.shape[0]
+
+    loads = [
+        pltpu.make_async_copy(gate, gate_v, local_sem.at[0]),
+        pltpu.make_async_copy(up, up_v, local_sem.at[1]),
+        pltpu.make_async_copy(tokens, tok.at[z], local_sem.at[2]),
+        pltpu.make_async_copy(down, down_v, local_sem.at[3]),
+        pltpu.make_async_copy(proj, proj_v, local_sem.at[4]),
+        pltpu.make_async_copy(queries, q_all.at[x], local_sem.at[5]),
+    ]
+    for load in loads:
+        load.start()
+
+    barrier = pltpu.get_barrier_semaphore()
+    partners = [{"expert": lax.rem(z + k, n_exp)} for k in range(1, n_exp)]
+    partners += [{"dp": 1 - c}, {"query": 1 - x}, {"group": 1 - y}, {"query": 1 - x, "dp": 1 - c}]
+    for who in partners:
+        pl.semaphore_signal(barrier, inc=1, device_id=who, device_id_type=MESH)
+
+    row_id = lax.broadcasted_iota(jnp.int32, comb.shape[1:], 0)
+    spread = jnp.zeros(comb.shape[1:], jnp.float32)
+    for k in range(top):
+        spread += jnp.where(routes[k : k + 1, :] == row_id, gates[k : k + 1, :], 0.0)
+    comb[z] = spread
+    pl.semaphore_wait(barrier, len(partners))
+
+    def remote(src, dst, ss, rs, who):
+        return pltpu.make_async_remote_copy(
+            src_ref=src, dst_ref=dst, send_sem=ss, recv_sem=rs, device_id=who, device_id_type=MESH
+        )
+
+    def tok_copy(step, owner, h, src=None):
+        part = pl.ds(h * piece, piece)
+        dst = tok.at[owner, part]
+        return remote(
+            dst if src is None else src.at[part],
+            dst,
+            tok_ss.at[(step + 1) // 2, owner, h],
+            tok_rs.at[owner, h],
+            {"expert": jnp.clip(z + step, 0, n_exp - 1)},
+        )
+
+    for h in range(PIECES):
+        pl.when(z + 1 < n_exp)(lambda h=h: tok_copy(1, z, h, tokens).start())
+        pl.when(z > 0)(lambda h=h: tok_copy(-1, z, h, tokens).start())
+
+    def comb_copy(k):
+        return remote(
+            comb.at[z], comb.at[z], comb_ss.at[k], comb_rs.at[z], {"expert": lax.rem(z + k, n_exp)}
+        )
+
+    for k in range(1, n_exp):
+        comb_copy(k).start()
+
+    own = 2 * x + c
+    other = 2 * (1 - x) + c
+    loads[0].wait()
+    loads[1].wait()
+    block = width // 8
+
+    def arrange(i, _):
+        part = pl.ds(i * block, block)
+        g, u = gate_v[part, :], up_v[part, :]
+        w_all[own, part, :full] = g[:, :full]
+        w_all[own, part, full : 2 * full] = u[:, :full]
+        w_all[own, part, 2 * full :] = jnp.concatenate([g[:, full:], u[:, full:]], axis=1)
+        return 0
+
+    lax.fori_loop(0, 8, arrange, 0)
+
+    def w_part(side, k):
+        return pl.ds(side * half_rows + k * w_rows, w_rows)
+
+    def wx_copy(k):
+        part = w_part(y, k)
+        ref = w_all.at[own, part]
+        return remote(ref, ref, wx_ss.at[k], wx_rs.at[k], {"query": 1 - x})
+
+    def wy_copy(k):
+        ref = w_all.at[other, w_part(y, k)]
+        return remote(ref, ref, wy_ss.at[k], wy_rs.at[k], {"group": 1 - y})
+
+    def wd_copy(from_y, k):
+        ref = w_all.at[other, w_part(1 - y if from_y else y, k)]
+        return remote(ref, ref, wd_ss.at[from_y, k], wd_rs.at[from_y, k], {"dp": 1 - c})
+
+    own_copy = remote(w_all.at[own], w_all.at[own], own_ss, own_rs, {"dp": 1 - c})
+
+    for k in range(W_PIECES):
+        wx_copy(k).start()
+    own_copy.start()
+
+    loads[3].wait()
+    loads[4].wait()
+    folded = lax.dot_general(
+        down_v[...], proj_v[...], (((0,), (0,)), ((), ())), preferred_element_type=jnp.float32
+    )
+    high = folded.astype(jnp.bfloat16)
+    low = (folded - high.astype(jnp.float32)).astype(jnp.bfloat16)
+    out_width = proj.shape[1]
+    pad_rows = v_all.shape[1] - units
+    v_all[own, :units, :out_width] = high
+    v_all[own, :units, out_width:] = low
+    v_all[own, units:, :] = jnp.zeros((pad_rows, 2 * out_width), jnp.bfloat16)
+
+    loads[2].wait()
+    base[...] = jnp.dot(tok[z], proj_v[...], preferred_element_type=jnp.float32)
+
+    v_to = [{"dp": 1 - c}, {"query": 1 - x}, {"query": 1 - x, "dp": 1 - c}]
+    v_copies = [remote(v_all.at[own], v_all.at[own], v_ss.at[i], v_rs.at[i], who) for i, who in enumerate(v_to)]
+    for copy in v_copies:
+        copy.start()
+    q_copy = remote(queries, q_all.at[x], q_ss, q_rs, {"query": 1 - x})
+    q_copy.start()
+
+    def expert_rows(owner, first, count, expert, halves_from):
+        rows_in = tok[owner, pl.ds(first, count), :]
+        pick = jnp.sum(
+            jnp.where(row_id == z * 2 + expert, comb[owner], 0.0), axis=0, keepdims=True
+        )
+        scale = jnp.broadcast_to(pick, (out_width, rows)).T[first : first + count]
+
+        def one(c_at, total):
+            j = 2 * expert + c_at
+            act = jnp.dot(rows_in, w_all[j], preferred_element_type=jnp.float32)
+            g, u = act[:, :full], act[:, full : 2 * full]
+            t = act[:, 2 * full :]
+            main = g / (1.0 + jnp.exp(-g)) * u
+            last = t / (1.0 + jnp.exp(-t)) * pltpu.roll(t, LANES // 2, 1)
+            hidden = jnp.concatenate([main, last], axis=1).astype(jnp.bfloat16)
+            both = jnp.dot(hidden, v_all[j], preferred_element_type=jnp.float32)
+            return total + (both[:, :out_width] + both[:, out_width:])
+
+        total = lax.fori_loop(0, 2, one, jnp.zeros((count, out_width), jnp.float32))
+        return total * scale
+
+    own_copy.wait_recv()
+    v_copies[0].wait_recv()
+    acc[z] = expert_rows(z, 0, rows, x, 0)
+
+    def take(d, h):
+        for side in (-1, 1):
+            owner = jnp.clip(z + side * d, 0, n_exp - 1)
+            inside = (z - d >= 0) if side < 0 else (z + d < n_exp)
+
+            def arrive(side=side, owner=owner):
+                tok_copy(1, owner, h).wait_recv()
+
+                if d < n_exp - 1:
+                    onward = (z + 1 < n_exp) if side < 0 else (z > 0)
+                    pl.when(onward)(lambda: tok_copy(-side, owner, h).start())
+
+            pl.when(inside)(arrive)
+
+    def comb_wait(k):
+        src = lax.rem(z + n_exp - k, n_exp)
+        remote(
+            comb.at[src], comb.at[src], comb_ss.at[k], comb_rs.at[src], {"expert": src}
+        ).wait_recv()
+
+    for k in range(1, n_exp):
+        comb_wait(k)
+
+    x_taken = 0
+
+    def take_x(k):
+        part = w_part(y, k)
+        remote(
+            w_all.at[other, part], w_all.at[other, part], wx_ss.at[k], wx_rs.at[k], {"query": 1 - x}
+        ).wait_recv()
+        wy_copy(k).start()
+        wd_copy(0, k).start()
+
+    for d in range(1, n_exp - 1):
+        for h in range(PIECES):
+            take(d, h)
+            if (d > 1 or h == PIECES - 1) and x_taken < W_PIECES:
+                take_x(x_taken)
+                x_taken += 1
+
+        def near(owner, _, d=d):
+            @pl.when(jnp.abs(owner - z) == d)
+            def _():
+                acc[owner] = expert_rows(owner, 0, rows, x, 0)
+
+            return 0
+
+        lax.fori_loop(0, n_exp, near, 0)
+    while x_taken < W_PIECES:
+        take_x(x_taken)
+        x_taken += 1
+
+    for k in range(W_PIECES):
+        part = w_part(1 - y, k)
+        ref = w_all.at[other, part]
+        remote(ref, ref, wy_ss.at[k], wy_rs.at[k], {"group": 1 - y}).wait_recv()
+        wd_copy(1, k).start()
+    peer = 2 * (1 - x) + 1 - c
+    for from_y in range(2):
+        for k in range(W_PIECES):
+            ref = w_all.at[peer, w_part(1 - y if from_y else y, k)]
+            remote(ref, ref, wd_ss.at[from_y, k], wd_rs.at[from_y, k], {"dp": 1 - c}).wait_recv()
+    v_copies[1].wait_recv()
+    v_copies[2].wait_recv()
+
+    def far(owner, _):
+        @pl.when(jnp.abs(owner - z) < n_exp - 1)
+        def _():
+            acc[owner] += expert_rows(owner, 0, rows, 1 - x, 0)
+
+        return 0
+
+    lax.fori_loop(0, n_exp, far, 0)
+
+    def ret_copy(owner, h):
+        part = pl.ds(h * piece, piece)
+        return remote(
+            acc.at[owner, part],
+            ret.at[z, part],
+            ret_ss.at[owner, h],
+            ret_rs.at[z, h],
+            {"expert": owner},
+        )
+
+    def ret_wait(src, h):
+        part = pl.ds(h * piece, piece)
+        remote(
+            acc.at[src, part], ret.at[src, part], ret_ss.at[src, h], ret_rs.at[src, h], {"expert": src}
+        ).wait_recv()
+
+    for owner in range(n_exp):
+        @pl.when(jnp.logical_and(jnp.abs(owner - z) < n_exp - 1, owner != z))
+        def _(owner=owner):
+            for h in range(PIECES):
+                ret_copy(owner, h).start()
+
+    @pl.when(jnp.logical_or(z == 0, z == n_exp - 1))
+    def _():
+        owner = n_exp - 1 - z
+        for h in range(PIECES):
+            tok_copy(1, owner, h).wait_recv()
+
+            def add(e, total, h=h):
+                return total + expert_rows(owner, h * piece, piece, e, 0)
+
+            acc[owner, pl.ds(h * piece, piece)] = lax.fori_loop(
+                0, 2, add, jnp.zeros((piece, out_width), jnp.float32)
+            )
+            ret_copy(owner, h).start()
+
+    loads[5].wait()
+    q_in = remote(queries, q_all.at[1 - x], q_ss, q_rs, {"query": 1 - x})
+    q_in.wait_recv()
+
+    base[...] += acc[z]
+    for dist in range(1, n_exp):
+        for side in (-1, 1):
+            src = z + side * dist
+            inside = (src >= 0) if side < 0 else (src < n_exp)
+
+            @pl.when(inside)
+            def _(src=jnp.clip(src, 0, n_exp - 1)):
+                for h in range(PIECES):
+                    ret_wait(src, h)
+                base[...] += ret[src]
+
+    projected = base[...]
+    norm = jnp.sqrt(jnp.sum(projected * projected, axis=-1, keepdims=True) + 1e-06)
+    embedding = (projected / norm).astype(jnp.bfloat16)
+    n_pass, n_lab = out.shape
+    n_blocks, q_rows = q_all.shape[0], q_all.shape[1]
+    q_len = q_rows * n_blocks // n_lab
+    token_at = lax.broadcasted_iota(jnp.int32, (PLEN, q_rows), 0)
+    label_at = lax.broadcasted_iota(jnp.int32, (q_rows, LANES), 0) // q_len
+    column = lax.broadcasted_iota(jnp.int32, (q_rows, LANES), 1)
+    total = jnp.zeros((3 * 8, LANES), jnp.float32)
+    for b in range(n_blocks):
+        raw = lax.dot_general(
+            embedding, q_all[b], (((1,), (1,)), ((), ())), preferred_element_type=jnp.float32
+        )
+        best = [
+            jnp.max(
+                jnp.where(token_at < plens[p], raw[p * PLEN : (p + 1) * PLEN], -jnp.inf),
+                axis=0,
+                keepdims=True,
+            )
+            for p in range(n_pass)
+        ]
+        best = jnp.concatenate(best + [jnp.zeros((8 - n_pass, q_rows), jnp.float32)], axis=0)
+        first = best.astype(jnp.bfloat16).astype(jnp.float32)
+        second = (best - first).astype(jnp.bfloat16).astype(jnp.float32)
+        third = best - first - second
+        parts = jnp.concatenate([first, second, third], axis=0).astype(jnp.bfloat16)
+        members = jnp.where(column == label_at + b * (n_lab // n_blocks), 1.0, 0.0).astype(jnp.bfloat16)
+        total += jnp.dot(parts, members, preferred_element_type=jnp.float32)
+    summed = total[0:8] + total[8:16] + total[16:24]
+    out[...] = summed[:n_pass, :n_lab]
+
+    for h in range(PIECES):
+        for owner in range(n_exp):
+            @pl.when(jnp.logical_and(z + 1 < n_exp, owner <= z))
+            def _(owner=owner, h=h):
+                tok_copy(1, owner, h).wait_send()
+
+            @pl.when(jnp.logical_and(z > 0, owner >= z))
+            def _(owner=owner, h=h):
+                tok_copy(-1, owner, h).wait_send()
+
+            @pl.when(owner != z)
+            def _(owner=owner, h=h):
+                ret_copy(owner, h).wait_send()
+
+    for k in range(1, n_exp):
+        comb_copy(k).wait_send()
+    for k in range(W_PIECES):
+        wx_copy(k).wait_send()
+        wy_copy(k).wait_send()
+        wd_copy(0, k).wait_send()
+        wd_copy(1, k).wait_send()
+    own_copy.wait_send()
+    for copy in v_copies:
+        copy.wait_send()
+    q_copy.wait_send()
+
+
+def dense_on_device(
+    n_exp,
+    tokens,
+    route_ids,
+    gate_values,
+    passage_lengths,
+    gate_weight,
+    up_weight,
+    down_weight,
+    proj_weight,
+    queries,
+):
+    rows, width = tokens.shape
+    units = gate_weight.shape[2]
+    out_width = proj_weight.shape[1]
+    queries2 = queries.reshape(-1, queries.shape[-1])
+    n_experts = n_exp * 2
+    v_rows = (units // LANES + 1) * LANES
+    any_spec = pl.BlockSpec(memory_space=pl.ANY)
+    vmem_spec = pl.BlockSpec(memory_space=pltpu.VMEM)
+    dma = pltpu.SemaphoreType.DMA
+    bf16, f32 = jnp.bfloat16, jnp.float32
+    return pl.pallas_call(
+        functools.partial(dense_kernel, n_exp),
+        out_shape=jax.ShapeDtypeStruct((passage_lengths.shape[0], queries.shape[0] * 2), f32),
+        in_specs=[any_spec] * 6 + [vmem_spec] * 2 + [pl.BlockSpec(memory_space=pltpu.SMEM)],
+        out_specs=vmem_spec,
+        scratch_shapes=[
+            pltpu.VMEM((n_exp, rows, width), bf16),
+            pltpu.VMEM((width, units), bf16),
+            pltpu.VMEM((width, units), bf16),
+            pltpu.VMEM((width, units), bf16),
+            pltpu.VMEM((width, out_width), bf16),
+            pltpu.VMEM((4, width, 2 * units), bf16),
+            pltpu.VMEM((4, v_rows, 2 * out_width), bf16),
+            pltpu.VMEM((2,) + queries2.shape, bf16),
+            pltpu.VMEM((n_exp, n_experts, rows), f32),
+            pltpu.VMEM((n_exp, rows, out_width), f32),
+            pltpu.VMEM((n_exp, rows, out_width), f32),
+            pltpu.VMEM((rows, out_width), f32),
+            dma((6,)),
+            dma((2, n_exp, PIECES)),
+            dma((n_exp, PIECES)),
+            dma((n_exp,)),
+            dma((n_exp,)),
+            dma,
+            dma,
+            dma((W_PIECES,)),
+            dma((W_PIECES,)),
+            dma((W_PIECES,)),
+            dma((W_PIECES,)),
+            dma((2, W_PIECES)),
+            dma((2, W_PIECES)),
+            dma((3,)),
+            dma((3,)),
+            dma,
+            dma,
+            dma((n_exp, PIECES)),
+            dma((n_exp, PIECES)),
+        ],
+        compiler_params=pltpu.CompilerParams(collective_id=0, has_side_effects=True),
+    )(
+        tokens,
+        gate_weight[0],
+        up_weight[0],
+        down_weight[0],
+        proj_weight,
+        queries2,
+        route_ids.T,
+        gate_values.T,
+        passage_lengths,
+    )
+
+
+def dense_fits(mesh_shape, rows, units, top):
+    experts = mesh_shape["expert"] * mesh_shape["query"]
+    pairs = all(mesh_shape[a] == 2 for a in ("group", "query", "dp"))
+    capacity = max(2, 2 * rows * top // experts)
+    return pairs and mesh_shape["expert"] > 2 and capacity >= rows and units % LANES == LANES // 2
 
 
 def passage_scores(embedding, live_mask, block_queries):
@@ -100,6 +574,14 @@
         P(("group", "query"), None, None),
     )
     out_specs = P(("group", "expert", "query", "dp"), None)
+    sizes = dict(mesh.shape)
+
+    def run(tokens, route_ids, *rest):
+        units = rest[2].shape[2]
+        if dense_fits(sizes, tokens.shape[0], units, route_ids.shape[1]):
+            return dense_on_device(sizes["expert"], tokens, route_ids, *rest)
+        return on_device(tokens, route_ids, *rest)
+
     return jax.shard_map(
-        on_device, mesh=mesh, in_specs=in_specs, out_specs=out_specs, check_vma=False
-    )
+        run, mesh=mesh, in_specs=in_specs, out_specs=out_specs, check_vma=False
+    )

time: 164 us -> 59.5 us (0.36); the launches traced: 162 us -> 59.3 us
  waiting for transfers between devices: 93.6 us -> 0 us
  Pallas kernels: 0 us -> 53.2 us
  matrix products: 16.6 us -> 0 us
  between operations: 13.3 us -> 0.01 us
  blocking collectives: 12 us -> 0 us
  starting transfers between devices: 11.1 us -> 0 us
  local copies, waits for them, and re-layouts: 12.6 us -> 6.13 us
  other arithmetic: 2.88 us -> 0 us
    all_to_all x2 -> x0, waiting for transfers between devices: 79.4 us -> none  [the longest x1 78.2 us: on_device(): lax.all_to_all(outgoing, ('expert', 'query'), split_axis=0, concat_axis=0...]
    pallas_call x0 -> x1, Pallas kernels: none -> 53.2 us  [dense_on_device(): pl.pallas_call(functools.partial(dense_kernel, n_exp), out_shape=jax.Shap...]
    dot_general x5 -> x0, matrix products: 16.6 us -> none  [the longest x1 5.7 us: on_device(): folded = jnp.dot(results, proj_weight, preferred_element_type=jnp.float32)]
    all_gather x3 -> x0, waiting for transfers between devices: 12.1 us -> none  [the longest x1 12.1 us: on_device(): lax.all_gather(gate_weight[0], 'dp', axis=1, tiled=True)]
    all_gather x1 -> x0, blocking collectives: 12 us -> none  [on_device(): lax.all_gather(queries, 'query', axis=0, tiled=True)]
    all_to_all x2 -> x0, starting transfers between devices: 11 us -> none  [the longest x1 6.34 us: on_device(): lax.all_to_all(outgoing, ('expert', 'query'), split_axis=0, concat_axis=0...]
    gather x2 -> x0, local copies, waits for them, and re-layouts: 7.05 us -> none  [the longest x1 6.03 us: on_device(): outgoing = padded[source_row].reshape(experts, capacity, model_width)]
    unnamed x12 -> x8, local copies, waits for them, and re-layouts: 0.99 us -> 6.13 us
  transfers between devices with their start and end apart: 5 -> 0, of which waited for: 3 -> 0; matrix products, arithmetic and copies ran while one was open for 6% -> 0% of each run, Pallas kernels for 0% -> 0%
where the time goes in v1:
time: 59.5 us; the launch traced here: 59.3 us
  Pallas kernels  53.2 us (89%)
  local copies, waits for them, and re-layouts  6.13 us (10%)
    pallas_call x1, Pallas kernels, dense_on_device(): pl.pallas_call(functools.partial(dense_kernel, n_exp), out_shape=jax.Shap...  53.2 us
    unnamed x8, local copies, waits for them, and re-layouts  6.13 us

profile of v1, /device:TPU:1, one launch (start us, length us, event | category | flops | bytes accessed | tf_op | source)
XLA Modules:
  0.0 59.3 jit_solution(11100384737154102394)
XLA Ops:
  0.0 0.0 copy-start
  0.0 2.3 %copy.10 = bf16[1,2048,192]{2,1,0:T(8,128)(2,1)} copy(bf16[1,2048,192]{1,2,0:T(8,128)(2,1)} %param.13) | data formatting | bytes 1572864 | tf_op args[4]
  2.3 0.0 copy-done
  2.3 0.0 copy-start.1
  2.3 1.3 %copy.11 = bf16[1,2048,192]{2,1,0:T(8,128)(2,1)} copy(bf16[1,2048,192]{1,2,0:T(8,128)(2,1)S(1)} %copy-done) | data formatting | bytes 1572864 | tf_op args[5]
  3.6 0.0 copy-done.1
  3.6 1.3 %copy.12 = bf16[1,2048,192]{2,1,0:T(8,128)(2,1)} copy(bf16[1,2048,192]{1,2,0:T(8,128)(2,1)S(1)} %copy-done.1) | data formatting | bytes 1572864 | tf_op args[6]
  4.9 53.2 %shard_map.91 = f32[2,64]{1,0:T(2,128)} custom-call(bf16[128,2048]{1,0:T(8,128)(2,1)} %tokens.1, bf16[2048,192]{1,0:T(8,128)(2,1)} %bitcast.6, bf16[2048,192]{1,0:T(8,128)(2,1)} %bitcast.7, bf16[2048,192]{1,0:T(8,128)(2,1)} %bitcast.8, bf16[2048,128]{1,0:T(8,128)(2,1)} %proj.1, bf16[1024,128]{1,0:T(8,128)(2,1)} %bitcast.9, s32[4,128]{1,0:T(4,128)} %bitcast.10, ...), custom_call_target="tpu_custom_call" | custom-call | tf_op jit(solution)/shard_map/pallas_call | solution.py:424
  58.1 1.2 %copy.14 = f32[2,64]{1,0:T(2,128)} copy(f32[2,64]{1,0:T(2,128)} %shard_map.91) | data formatting | bytes 1024
Async XLA Ops:
  0.0 2.3 %copy-start = (bf16[1,2048,192]{1,2,0:T(8,128)(2,1)S(1)}, bf16[1,2048,192]{1,2,0:T(8,128)(2,1)}, u32[]{:S(2)}) copy-start(bf16[1,2048,192]{1,2,0:T(8,128)(2,1)} %param.14) | copy-start | bytes 2359300
  2.3 1.3 %copy-start.1 = (bf16[1,2048,192]{1,2,0:T(8,128)(2,1)S(1)}, bf16[1,2048,192]{1,2,0:T(8,128)(2,1)}, u32[]{:S(2)}) copy-start(bf16[1,2048,192]{1,2,0:T(8,128)(2,1)} %param.15) | copy-start | bytes 2359300

commit v2 on v1

--- a/solution.py
+++ b/solution.py
@@ -10,16 +10,8 @@
 PLEN = 64
 MESH = pl.DeviceIdType.MESH
 LANES = 128
-PIECES = 2
-W_PIECES = 2
-
-
-def when_all(conds, body):
-    live = [c for c in conds if c is not None]
-    if live:
-        pl.when(functools.reduce(jnp.logical_and, live))(body)
-    else:
-        body()
+PIECES = 4
+W_PIECES = 4
 
 
 def dense_kernel(
@@ -35,8 +27,6 @@
     plens,
     out,
     tok,
-    gate_v,
-    up_v,
     down_v,
     proj_v,
     w_all,
@@ -46,6 +36,8 @@
     acc,
     ret,
     base,
+    part_act,
+    members,
     local_sem,
     tok_ss,
     tok_rs,
@@ -69,20 +61,29 @@
     z, x = lax.axis_index("expert"), lax.axis_index("query")
     y, c = lax.axis_index("group"), lax.axis_index("dp")
     rows, width = tokens.shape
-    units = gate.shape[1]
+    units = gate.shape[0]
     full = units // LANES * LANES
-    piece = rows // PIECES
-    half_rows = width // 2
+    piece = width // PIECES
+    half_rows = units
     w_rows = half_rows // W_PIECES
+    own = 2 * x + c
+    other = 2 * (1 - x) + c
+    ends = 2 * full + units - full
     top = routes.shape[0]
 
+    w_own = w_all.at[own]
+    arranged = [
+        (gate.at[:full], w_own.at[:full]),
+        (up.at[:full], w_own.at[full : 2 * full]),
+        (gate.at[full:], w_own.at[2 * full : ends]),
+        (up.at[full:], w_own.at[ends:]),
+        (tokens, tok.at[z]),
+        (down, down_v),
+        (proj, proj_v),
+        (queries, q_all.at[x]),
+    ]
     loads = [
-        pltpu.make_async_copy(gate, gate_v, local_sem.at[0]),
-        pltpu.make_async_copy(up, up_v, local_sem.at[1]),
-        pltpu.make_async_copy(tokens, tok.at[z], local_sem.at[2]),
-        pltpu.make_async_copy(down, down_v, local_sem.at[3]),
-        pltpu.make_async_copy(proj, proj_v, local_sem.at[4]),
-        pltpu.make_async_copy(queries, q_all.at[x], local_sem.at[5]),
+        pltpu.make_async_copy(src, dst, local_sem.at[i]) for i, (src, dst) in enumerate(arranged)
     ]
     for load in loads:
         load.start()
@@ -107,9 +108,9 @@
 
     def tok_copy(step, owner, h, src=None):
         part = pl.ds(h * piece, piece)
-        dst = tok.at[owner, part]
+        dst = tok.at[owner, :, part]
         return remote(
-            dst if src is None else src.at[part],
+            dst if src is None else src.at[:, part],
             dst,
             tok_ss.at[(step + 1) // 2, owner, h],
             tok_rs.at[owner, h],
@@ -128,21 +129,8 @@
     for k in range(1, n_exp):
         comb_copy(k).start()
 
-    own = 2 * x + c
-    other = 2 * (1 - x) + c
-    loads[0].wait()
-    loads[1].wait()
-    block = width // 8
-
-    def arrange(i, _):
-        part = pl.ds(i * block, block)
-        g, u = gate_v[part, :], up_v[part, :]
-        w_all[own, part, :full] = g[:, :full]
-        w_all[own, part, full : 2 * full] = u[:, :full]
-        w_all[own, part, 2 * full :] = jnp.concatenate([g[:, full:], u[:, full:]], axis=1)
-        return 0
-
-    lax.fori_loop(0, 8, arrange, 0)
+    for i in range(4):
+        loads[i].wait()
 
     def w_part(side, k):
         return pl.ds(side * half_rows + k * w_rows, w_rows)
@@ -166,11 +154,9 @@
         wx_copy(k).start()
     own_copy.start()
 
-    loads[3].wait()
-    loads[4].wait()
-    folded = lax.dot_general(
-        down_v[...], proj_v[...], (((0,), (0,)), ((), ())), preferred_element_type=jnp.float32
-    )
+    loads[5].wait()
+    loads[6].wait()
+    folded = jnp.dot(down_v[...], proj_v[...], preferred_element_type=jnp.float32)
     high = folded.astype(jnp.bfloat16)
     low = (folded - high.astype(jnp.float32)).astype(jnp.bfloat16)
     out_width = proj.shape[1]
@@ -179,7 +165,7 @@
     v_all[own, :units, out_width:] = low
     v_all[own, units:, :] = jnp.zeros((pad_rows, 2 * out_width), jnp.bfloat16)
 
-    loads[2].wait()
+    loads[4].wait()
     base[...] = jnp.dot(tok[z], proj_v[...], preferred_element_type=jnp.float32)
 
     v_to = [{"dp": 1 - c}, {"query": 1 - x}, {"query": 1 - x, "dp": 1 - c}]
@@ -189,30 +175,40 @@
     q_copy = remote(queries, q_all.at[x], q_ss, q_rs, {"query": 1 - x})
     q_copy.start()
 
-    def expert_rows(owner, first, count, expert, halves_from):
-        rows_in = tok[owner, pl.ds(first, count), :]
+    def product(owner, j, first, count):
+        return lax.dot_general(
+            tok[owner, :, first : first + count],
+            w_all[j, :, first : first + count],
+            (((1,), (1,)), ((), ())),
+            preferred_element_type=jnp.float32,
+        )
+
+    def after(act, j):
+        g, u = act[:, :full], act[:, full : 2 * full]
+        t = act[:, 2 * full :]
+        main = g / (1.0 + jnp.exp(-g)) * u
+        last = t / (1.0 + jnp.exp(-t)) * pltpu.roll(t, LANES // 2, 1)
+        hidden = jnp.concatenate([main, last], axis=1).astype(jnp.bfloat16)
+        both = jnp.dot(hidden, v_all[j], preferred_element_type=jnp.float32)
+        return both[:, :out_width] + both[:, out_width:]
+
+    def scale_of(owner, expert):
         pick = jnp.sum(
             jnp.where(row_id == z * 2 + expert, comb[owner], 0.0), axis=0, keepdims=True
         )
-        scale = jnp.broadcast_to(pick, (out_width, rows)).T[first : first + count]
-
+        return jnp.broadcast_to(pick, (out_width, rows)).T
+
+    def expert_rows(owner, expert):
         def one(c_at, total):
             j = 2 * expert + c_at
-            act = jnp.dot(rows_in, w_all[j], preferred_element_type=jnp.float32)
-            g, u = act[:, :full], act[:, full : 2 * full]
-            t = act[:, 2 * full :]
-            main = g / (1.0 + jnp.exp(-g)) * u
-            last = t / (1.0 + jnp.exp(-t)) * pltpu.roll(t, LANES // 2, 1)
-            hidden = jnp.concatenate([main, last], axis=1).astype(jnp.bfloat16)
-            both = jnp.dot(hidden, v_all[j], preferred_element_type=jnp.float32)
-            return total + (both[:, :out_width] + both[:, out_width:])
-
-        total = lax.fori_loop(0, 2, one, jnp.zeros((count, out_width), jnp.float32))
-        return total * scale
+            return total + after(product(owner, j, 0, width), j)
+
+        total = lax.fori_loop(0, 2, one, jnp.zeros((rows, out_width), jnp.float32))
+        return total * scale_of(owner, expert)
 
     own_copy.wait_recv()
     v_copies[0].wait_recv()
-    acc[z] = expert_rows(z, 0, rows, x, 0)
+    acc[z] = expert_rows(z, x)
 
     def take(d, h):
         for side in (-1, 1):
@@ -250,14 +246,14 @@
     for d in range(1, n_exp - 1):
         for h in range(PIECES):
             take(d, h)
-            if (d > 1 or h == PIECES - 1) and x_taken < W_PIECES:
+            if h % 2 == (1 if d == 1 else 0) and x_taken < W_PIECES:
                 take_x(x_taken)
                 x_taken += 1
 
         def near(owner, _, d=d):
             @pl.when(jnp.abs(owner - z) == d)
             def _():
-                acc[owner] = expert_rows(owner, 0, rows, x, 0)
+                acc[owner] = expert_rows(owner, x)
 
             return 0
 
@@ -282,53 +278,67 @@
     def far(owner, _):
         @pl.when(jnp.abs(owner - z) < n_exp - 1)
         def _():
-            acc[owner] += expert_rows(owner, 0, rows, 1 - x, 0)
+            acc[owner] += expert_rows(owner, 1 - x)
 
         return 0
 
     lax.fori_loop(0, n_exp, far, 0)
 
-    def ret_copy(owner, h):
-        part = pl.ds(h * piece, piece)
+    def ret_copy(owner):
         return remote(
-            acc.at[owner, part],
-            ret.at[z, part],
-            ret_ss.at[owner, h],
-            ret_rs.at[z, h],
-            {"expert": owner},
-        )
-
-    def ret_wait(src, h):
-        part = pl.ds(h * piece, piece)
+            acc.at[owner], ret.at[z], ret_ss.at[owner], ret_rs.at[z], {"expert": owner}
+        )
+
+    def ret_wait(src):
         remote(
-            acc.at[src, part], ret.at[src, part], ret_ss.at[src, h], ret_rs.at[src, h], {"expert": src}
+            acc.at[src], ret.at[src], ret_ss.at[src], ret_rs.at[src], {"expert": src}
         ).wait_recv()
 
     for owner in range(n_exp):
         @pl.when(jnp.logical_and(jnp.abs(owner - z) < n_exp - 1, owner != z))
         def _(owner=owner):
-            for h in range(PIECES):
-                ret_copy(owner, h).start()
+            ret_copy(owner).start()
+
+    n_pass, n_lab = out.shape
+    n_blocks, q_rows = q_all.shape[0], q_all.shape[1]
+    q_len = q_rows * n_blocks // n_lab
+    label_at = lax.broadcasted_iota(jnp.int32, (q_rows, LANES), 0) // q_len
+    column = lax.broadcasted_iota(jnp.int32, (q_rows, LANES), 1)
+    for b in range(n_blocks):
+        members[b] = jnp.where(column == label_at + b * (n_lab // n_blocks), 1.0, 0.0).astype(
+            jnp.bfloat16
+        )
+    base[...] += acc[z]
 
     @pl.when(jnp.logical_or(z == 0, z == n_exp - 1))
     def _():
         owner = n_exp - 1 - z
+        scales = [scale_of(owner, e) for e in range(2)]
         for h in range(PIECES):
             tok_copy(1, owner, h).wait_recv()
-
-            def add(e, total, h=h):
-                return total + expert_rows(owner, h * piece, piece, e, 0)
-
-            acc[owner, pl.ds(h * piece, piece)] = lax.fori_loop(
-                0, 2, add, jnp.zeros((piece, out_width), jnp.float32)
-            )
-            ret_copy(owner, h).start()
-
-    loads[5].wait()
+            if h < PIECES - 1:
+
+                def more(j, _, h=h):
+                    term = product(owner, j, h * piece, piece)
+                    part_act[j] = term if h == 0 else part_act[j] + term
+                    return 0
+
+                lax.fori_loop(0, 4, more, 0)
+        total = None
+        for e in range(2):
+            term = None
+            for c_at in range(2):
+                j = 2 * e + c_at
+                act = part_act[j] + product(owner, j, width - piece, piece)
+                term = after(act, j) if term is None else term + after(act, j)
+            total = term * scales[e] if total is None else total + term * scales[e]
+        acc[owner] = total
+        ret_copy(owner).start()
+
+    loads[7].wait()
     q_in = remote(queries, q_all.at[1 - x], q_ss, q_rs, {"query": 1 - x})
     q_in.wait_recv()
 
-    base[...] += acc[z]
     for dist in range(1, n_exp):
         for side in (-1, 1):
             src = z + side * dist
@@ -336,39 +346,32 @@
 
             @pl.when(inside)
             def _(src=jnp.clip(src, 0, n_exp - 1)):
-                for h in range(PIECES):
-                    ret_wait(src, h)
+                ret_wait(src)
                 base[...] += ret[src]
 
     projected = base[...]
     norm = jnp.sqrt(jnp.sum(projected * projected, axis=-1, keepdims=True) + 1e-06)
-    embedding = (projected / norm).astype(jnp.bfloat16)
-    n_pass, n_lab = out.shape
-    n_blocks, q_rows = q_all.shape[0], q_all.shape[1]
-    q_len = q_rows * n_blocks // n_lab
-    token_at = lax.broadcasted_iota(jnp.int32, (PLEN, q_rows), 0)
-    label_at = lax.broadcasted_iota(jnp.int32, (q_rows, LANES), 0) // q_len
-    column = lax.broadcasted_iota(jnp.int32, (q_rows, LANES), 1)
+    scaled = projected / norm
+    token_at = lax.broadcasted_iota(jnp.int32, (PLEN, out_width), 0)
+    live = []
+    for p in range(n_pass):
+        block = scaled[p * PLEN : (p + 1) * PLEN]
+        live.append(jnp.where(token_at < plens[p], block, block[0:1]))
+    embedding = jnp.concatenate(live, axis=0).astype(jnp.bfloat16)
     total = jnp.zeros((3 * 8, LANES), jnp.float32)
     for b in range(n_blocks):
         raw = lax.dot_general(
             embedding, q_all[b], (((1,), (1,)), ((), ())), preferred_element_type=jnp.float32
         )
         best = [
-            jnp.max(
-                jnp.where(token_at < plens[p], raw[p * PLEN : (p + 1) * PLEN], -jnp.inf),
-                axis=0,
-                keepdims=True,
-            )
-            for p in range(n_pass)
+            jnp.max(raw[p * PLEN : (p + 1) * PLEN], axis=0, keepdims=True) for p in range(n_pass)
         ]
         best = jnp.concatenate(best + [jnp.zeros((8 - n_pass, q_rows), jnp.float32)], axis=0)
         first = best.astype(jnp.bfloat16).astype(jnp.float32)
         second = (best - first).astype(jnp.bfloat16).astype(jnp.float32)
         third = best - first - second
         parts = jnp.concatenate([first, second, third], axis=0).astype(jnp.bfloat16)
-        members = jnp.where(column == label_at + b * (n_lab // n_blocks), 1.0, 0.0).astype(jnp.bfloat16)
-        total += jnp.dot(parts, members, preferred_element_type=jnp.float32)
+        total += jnp.dot(parts, members[b], preferred_element_type=jnp.float32)
     summed = total[0:8] + total[8:16] + total[16:24]
     out[...] = summed[:n_pass, :n_lab]
 
@@ -382,9 +385,10 @@
             def _(owner=owner, h=h):
                 tok_copy(-1, owner, h).wait_send()
 
-            @pl.when(owner != z)
-            def _(owner=owner, h=h):
-                ret_copy(owner, h).wait_send()
+    for owner in range(n_exp):
+        @pl.when(owner != z)
+        def _(owner=owner):
+            ret_copy(owner).wait_send()
 
     for k in range(1, n_exp):
         comb_copy(k).wait_send()
@@ -428,18 +432,18 @@
         out_specs=vmem_spec,
         scratch_shapes=[
             pltpu.VMEM((n_exp, rows, width), bf16),
-            pltpu.VMEM((width, units), bf16),
-            pltpu.VMEM((width, units), bf16),
-            pltpu.VMEM((width, units), bf16),
+            pltpu.VMEM((units, width), bf16),
             pltpu.VMEM((width, out_width), bf16),
-            pltpu.VMEM((4, width, 2 * units), bf16),
+            pltpu.VMEM((4, 2 * units, width), bf16),
             pltpu.VMEM((4, v_rows, 2 * out_width), bf16),
             pltpu.VMEM((2,) + queries2.shape, bf16),
             pltpu.VMEM((n_exp, n_experts, rows), f32),
             pltpu.VMEM((n_exp, rows, out_width), f32),
             pltpu.VMEM((n_exp, rows, out_width), f32),
             pltpu.VMEM((rows, out_width), f32),
-            dma((6,)),
+            pltpu.VMEM((4, rows, 2 * units), f32),
+            pltpu.VMEM((2, queries2.shape[0], LANES), bf16),
+            dma((8,)),
             dma((2, n_exp, PIECES)),
             dma((n_exp, PIECES)),
             dma((n_exp,)),
@@ -456,15 +460,15 @@
             dma((3,)),
             dma,
             dma,
-            dma((n_exp, PIECES)),
-            dma((n_exp, PIECES)),
+            dma((n_exp,)),
+            dma((n_exp,)),
         ],
         compiler_params=pltpu.CompilerParams(collective_id=0, has_side_effects=True),
     )(
         tokens,
-        gate_weight[0],
-        up_weight[0],
-        down_weight[0],
+        gate_weight[0].T,
+        up_weight[0].T,
+        down_weight[0].T,
         proj_weight,
         queries2,
         route_ids.T,

time: 59.5 us -> 55.8 us (0.938)
  local copies, waits for them, and re-layouts: 6.13 us -> 1.24 us
  Pallas kernels: 53.2 us -> 54.4 us
    unnamed x8 -> x1, local copies, waits for them, and re-layouts: 6.13 us -> 1.24 us
    pallas_call x1, Pallas kernels: 53.2 us -> 54.4 us  [dense_on_device(): pl.pallas_call(functools.partial(dense_kernel, n_exp), out_shape=jax.Shap...]
where the time goes in v2:
time: 55.8 us; the launch traced here: 55.7 us
  Pallas kernels  54.4 us (97%)
  local copies, waits for them, and re-layouts  1.24 us (2%)
    pallas_call x1, Pallas kernels, dense_on_device(): pl.pallas_call(functools.partial(dense_kernel, n_exp), out_shape=jax.Shap...  54.4 us
    unnamed x1, local copies, waits for them, and re-layouts  1.24 us

profile of v2, /device:TPU:1, one launch (start us, length us, event | category | flops | bytes accessed | tf_op | source)
XLA Modules:
  0.0 55.7 jit_solution(16487931363822643196)
XLA Ops:
  0.0 54.4 %shard_map.91 = f32[2,64]{1,0:T(2,128)} custom-call(bf16[128,2048]{1,0:T(8,128)(2,1)} %tokens.1, bf16[192,2048]{1,0:T(8,128)(2,1)} %bitcast.12, bf16[192,2048]{1,0:T(8,128)(2,1)} %bitcast.13, bf16[192,2048]{1,0:T(8,128)(2,1)} %bitcast.14, bf16[2048,128]{1,0:T(8,128)(2,1)} %proj.1, bf16[1024,128]{1,0:T(8,128)(2,1)} %bitcast.15, s32[4,128]{1,0:T(4,128)} %bitcast.16, ...), custom_call_target="tpu_custom_call" | custom-call | tf_op jit(solution)/shard_map/pallas_call | solution.py:428
  54.4 1.2 %copy.11 = f32[2,64]{1,0:T(2,128)} copy(f32[2,64]{1,0:T(2,128)} %shard_map.91) | data formatting | bytes 1024

commit v3 on v2

--- a/solution.py
+++ b/solution.py
@@ -90,7 +90,7 @@
 
     barrier = pltpu.get_barrier_semaphore()
     partners = [{"expert": lax.rem(z + k, n_exp)} for k in range(1, n_exp)]
-    partners += [{"dp": 1 - c}, {"query": 1 - x}, {"group": 1 - y}, {"query": 1 - x, "dp": 1 - c}]
+    partners += [{"dp": 1 - c}, {"query": 1 - x}, {"group": 1 - y}]
     for who in partners:
         pl.semaphore_signal(barrier, inc=1, device_id=who, device_id_type=MESH)
 
@@ -168,10 +168,12 @@
     loads[4].wait()
     base[...] = jnp.dot(tok[z], proj_v[...], preferred_element_type=jnp.float32)
 
-    v_to = [{"dp": 1 - c}, {"query": 1 - x}, {"query": 1 - x, "dp": 1 - c}]
-    v_copies = [remote(v_all.at[own], v_all.at[own], v_ss.at[i], v_rs.at[i], who) for i, who in enumerate(v_to)]
-    for copy in v_copies:
-        copy.start()
+    v_copies = [
+        remote(v_all.at[at], v_all.at[at], v_ss.at[i], v_rs.at[i], who)
+        for i, (at, who) in enumerate([(own, {"dp": 1 - c}), (own, {"query": 1 - x}), (other, {"dp": 1 - c})])
+    ]
+    v_copies[0].start()
+    v_copies[1].start()
     q_copy = remote(queries, q_all.at[x], q_ss, q_rs, {"query": 1 - x})
     q_copy.start()
 
@@ -246,7 +248,7 @@
     for d in range(1, n_exp - 1):
         for h in range(PIECES):
             take(d, h)
-            if h % 2 == (1 if d == 1 else 0) and x_taken < W_PIECES:
+            if (h >= 1 if d == 1 else h == 1) and x_taken < W_PIECES:
                 take_x(x_taken)
                 x_taken += 1
 
@@ -262,6 +264,8 @@
         take_x(x_taken)
         x_taken += 1
 
+    v_copies[1].wait_recv()
+    v_copies[2].start()
     for k in range(W_PIECES):
         part = w_part(1 - y, k)
         ref = w_all.at[other, part]
@@ -272,7 +276,6 @@
         for k in range(W_PIECES):
             ref = w_all.at[peer, w_part(1 - y if from_y else y, k)]
             remote(ref, ref, wd_ss.at[from_y, k], wd_rs.at[from_y, k], {"dp": 1 - c}).wait_recv()
-    v_copies[1].wait_recv()
     v_copies[2].wait_recv()
 
     def far(owner, _):

time: 55.8 us -> 55.8 us (level)
  no operation moved by 1% of the time
where the time goes in v3:
time: 55.8 us; the launch traced here: 55.7 us
  Pallas kernels  54.4 us (97%)
  local copies, waits for them, and re-layouts  1.24 us (2%)
    pallas_call x1, Pallas kernels, dense_on_device(): pl.pallas_call(functools.partial(dense_kernel, n_exp), out_shape=jax.Shap...  54.4 us
    unnamed x1, local copies, waits for them, and re-layouts  1.24 us

profile of v3, /device:TPU:1, one launch (start us, length us, event | category | flops | bytes accessed | tf_op | source)
XLA Modules:
  0.0 55.7 jit_solution(11831321535983838415)
XLA Ops:
  0.0 54.4 %shard_map.91 = f32[2,64]{1,0:T(2,128)} custom-call(bf16[128,2048]{1,0:T(8,128)(2,1)} %tokens.1, bf16[192,2048]{1,0:T(8,128)(2,1)} %bitcast.12, bf16[192,2048]{1,0:T(8,128)(2,1)} %bitcast.13, bf16[192,2048]{1,0:T(8,128)(2,1)} %bitcast.14, bf16[2048,128]{1,0:T(8,128)(2,1)} %proj.1, bf16[1024,128]{1,0:T(8,128)(2,1)} %bitcast.15, s32[4,128]{1,0:T(4,128)} %bitcast.16, ...), custom_call_target="tpu_custom_call" | custom-call | tf_op jit(solution)/shard_map/pallas_call | solution.py:431
  54.4 1.2 %copy.11 = f32[2,64]{1,0:T(2,128)} copy(f32[2,64]{1,0:T(2,128)} %shard_map.91) | data formatting | bytes 1024

commit v4 on v3

--- a/solution.py
+++ b/solution.py
@@ -89,17 +89,23 @@
         load.start()
 
     barrier = pltpu.get_barrier_semaphore()
-    partners = [{"expert": lax.rem(z + k, n_exp)} for k in range(1, n_exp)]
-    partners += [{"dp": 1 - c}, {"query": 1 - x}, {"group": 1 - y}]
+    partners = [{"dp": 1 - c}, {"query": 1 - x}, {"group": 1 - y}]
     for who in partners:
         pl.semaphore_signal(barrier, inc=1, device_id=who, device_id_type=MESH)
+    beside = [(z + 1 < n_exp, {"expert": z + 1}), (z > 0, {"expert": z - 1})]
+    for there, who in beside:
+
+        @pl.when(there)
+        def _(who=who):
+            pl.semaphore_signal(barrier, inc=1, device_id=who, device_id_type=MESH)
 
     row_id = lax.broadcasted_iota(jnp.int32, comb.shape[1:], 0)
     spread = jnp.zeros(comb.shape[1:], jnp.float32)
     for k in range(top):
         spread += jnp.where(routes[k : k + 1, :] == row_id, gates[k : k + 1, :], 0.0)
     comb[z] = spread
-    pl.semaphore_wait(barrier, len(partners))
+    at_end = jnp.logical_or(z == 0, z == n_exp - 1)
+    pl.semaphore_wait(barrier, jnp.where(at_end, len(partners) + 1, len(partners) + 2))
 
     def remote(src, dst, ss, rs, who):
         return pltpu.make_async_remote_copy(
@@ -121,13 +127,18 @@
         pl.when(z + 1 < n_exp)(lambda h=h: tok_copy(1, z, h, tokens).start())
         pl.when(z > 0)(lambda h=h: tok_copy(-1, z, h, tokens).start())
 
-    def comb_copy(k):
+    def comb_copy(step, owner):
+        ref = comb.at[owner]
         return remote(
-            comb.at[z], comb.at[z], comb_ss.at[k], comb_rs.at[z], {"expert": lax.rem(z + k, n_exp)}
-        )
-
-    for k in range(1, n_exp):
-        comb_copy(k).start()
+            ref,
+            ref,
+            comb_ss.at[(step + 1) // 2, owner],
+            comb_rs.at[owner],
+            {"expert": jnp.clip(z + step, 0, n_exp - 1)},
+        )
+
+    pl.when(z + 1 < n_exp)(lambda: comb_copy(1, z).start())
+    pl.when(z > 0)(lambda: comb_copy(-1, z).start())
 
     for i in range(4):
         loads[i].wait()
@@ -218,22 +229,14 @@
             inside = (z - d >= 0) if side < 0 else (z + d < n_exp)
 
             def arrive(side=side, owner=owner):
+                onward = (z + 1 < n_exp) if side < 0 else (z > 0)
                 tok_copy(1, owner, h).wait_recv()
-
-                if d < n_exp - 1:
-                    onward = (z + 1 < n_exp) if side < 0 else (z > 0)
-                    pl.when(onward)(lambda: tok_copy(-side, owner, h).start())
+                pl.when(onward)(lambda: tok_copy(-side, owner, h).start())
+                if h == 0:
+                    comb_copy(1, owner).wait_recv()
+                    pl.when(onward)(lambda: comb_copy(-side, owner).start())
 
             pl.when(inside)(arrive)
-
-    def comb_wait(k):
-        src = lax.rem(z + n_exp - k, n_exp)
-        remote(
-            comb.at[src], comb.at[src], comb_ss.at[k], comb_rs.at[src], {"expert": src}
-        ).wait_recv()
-
-    for k in range(1, n_exp):
-        comb_wait(k)
 
     x_taken = 0
 
@@ -278,14 +281,25 @@
             remote(ref, ref, wd_ss.at[from_y, k], wd_rs.at[from_y, k], {"dp": 1 - c}).wait_recv()
     v_copies[2].wait_recv()
 
-    def far(owner, _):
-        @pl.when(jnp.abs(owner - z) < n_exp - 1)
-        def _():
-            acc[owner] += expert_rows(owner, 1 - x)
-
-        return 0
-
-    lax.fori_loop(0, n_exp, far, 0)
+    many = n_exp - 1
+    start = jnp.where(z == n_exp - 1, 1, 0)
+    window = pl.ds(start, many)
+    rows_in = tok[window].reshape(many * rows, width)
+
+    def far(c_at, total):
+        j = 2 * (1 - x) + c_at
+        act = lax.dot_general(
+            rows_in, w_all[j], (((1,), (1,)), ((), ())), preferred_element_type=jnp.float32
+        )
+        return total + after(act, j)
+
+    total = lax.fori_loop(0, 2, far, jnp.zeros((many * rows, out_width), jnp.float32))
+    scales = jnp.concatenate([scale_of(start + i, 1 - x) for i in range(many)], axis=0)
+    acc[window] += (total * scales).reshape(many, rows, out_width)
+
+    @pl.when(jnp.logical_and(z > 0, z < n_exp - 1))
+    def _():
+        acc[n_exp - 1] += expert_rows(n_exp - 1, 1 - x)
 
     def ret_copy(owner):
         return remote(
@@ -316,6 +330,7 @@
     @pl.when(jnp.logical_or(z == 0, z == n_exp - 1))
     def _():
         owner = n_exp - 1 - z
+        comb_copy(1, owner).wait_recv()
         scales = [scale_of(owner, e) for e in range(2)]
         for h in range(PIECES):
             tok_copy(1, owner, h).wait_recv()
@@ -378,6 +393,13 @@
     summed = total[0:8] + total[8:16] + total[16:24]
     out[...] = summed[:n_pass, :n_lab]
 
+    for owner in range(n_exp):
+        pl.when(jnp.logical_and(z + 1 < n_exp, owner <= z))(
+            lambda owner=owner: comb_copy(1, owner).wait_send()
+        )
+        pl.when(jnp.logical_and(z > 0, owner >= z))(
+            lambda owner=owner: comb_copy(-1, owner).wait_send()
+        )
     for h in range(PIECES):
         for owner in range(n_exp):
             @pl.when(jnp.logical_and(z + 1 < n_exp, owner <= z))
@@ -393,8 +415,6 @@
         def _(owner=owner):
             ret_copy(owner).wait_send()
 
-    for k in range(1, n_exp):
-        comb_copy(k).wait_send()
     for k in range(W_PIECES):
         wx_copy(k).wait_send()
         wy_copy(k).wait_send()
@@ -449,7 +469,7 @@
             dma((8,)),
             dma((2, n_exp, PIECES)),
             dma((n_exp, PIECES)),
-            dma((n_exp,)),
+            dma((2, n_exp)),
             dma((n_exp,)),
             dma,
             dma,

time: 55.8 us -> 51.9 us (0.930)
  Pallas kernels: 54.4 us -> 50.5 us
    pallas_call x1, Pallas kernels: 54.4 us -> 50.5 us  [dense_on_device(): pl.pallas_call(functools.partial(dense_kernel, n_exp), out_shape=jax.Shap...]
where the time goes in v4:
time: 51.9 us; the launch traced here: 51.8 us
  Pallas kernels  50.5 us (97%)
  local copies, waits for them, and re-layouts  1.24 us (2%)
    pallas_call x1, Pallas kernels, dense_on_device(): pl.pallas_call(functools.partial(dense_kernel, n_exp), out_shape=jax.Shap...  50.5 us
    unnamed x1, local copies, waits for them, and re-layouts  1.24 us

profile of v4, /device:TPU:1, one launch (start us, length us, event | category | flops | bytes accessed | tf_op | source)
XLA Modules:
  0.0 51.8 jit_solution(14860489907817740794)
XLA Ops:
  0.0 50.5 %shard_map.91 = f32[2,64]{1,0:T(2,128)} custom-call(bf16[128,2048]{1,0:T(8,128)(2,1)} %tokens.1, bf16[192,2048]{1,0:T(8,128)(2,1)} %bitcast.12, bf16[192,2048]{1,0:T(8,128)(2,1)} %bitcast.13, bf16[192,2048]{1,0:T(8,128)(2,1)} %bitcast.14, bf16[2048,128]{1,0:T(8,128)(2,1)} %proj.1, bf16[1024,128]{1,0:T(8,128)(2,1)} %bitcast.15, s32[4,128]{1,0:T(4,128)} %bitcast.16, ...), custom_call_target="tpu_custom_call" | custom-call | tf_op jit(solution)/shard_map/pallas_call | solution.py:451
  50.5 1.2 %copy.11 = f32[2,64]{1,0:T(2,128)} copy(f32[2,64]{1,0:T(2,128)} %shard_map.91) | data formatting | bytes 1024

commit v5 on v4

--- a/solution.py
+++ b/solution.py
@@ -336,12 +336,9 @@
             tok_copy(1, owner, h).wait_recv()
             if h < PIECES - 1:
 
-                def more(j, _, h=h):
+                for j in range(4):
                     term = product(owner, j, h * piece, piece)
                     part_act[j] = term if h == 0 else part_act[j] + term
-                    return 0
-
-                lax.fori_loop(0, 4, more, 0)
         total = None
         for e in range(2):
             term = None

time: 51.9 us -> 50.7 us (0.977)
  Pallas kernels: 50.5 us -> 49.3 us
    pallas_call x1, Pallas kernels: 50.5 us -> 49.3 us  [dense_on_device(): pl.pallas_call(functools.partial(dense_kernel, n_exp), out_shape=jax.Shap...]
where the time goes in v5:
time: 50.7 us; the launch traced here: 50.5 us
  Pallas kernels  49.3 us (97%)
  local copies, waits for them, and re-layouts  1.24 us (2%)
    pallas_call x1, Pallas kernels, dense_on_device(): pl.pallas_call(functools.partial(dense_kernel, n_exp), out_shape=jax.Shap...  49.3 us
    unnamed x1, local copies, waits for them, and re-layouts  1.24 us

profile of v5, /device:TPU:1, one launch (start us, length us, event | category | flops | bytes accessed | tf_op | source)
XLA Modules:
  0.0 50.5 jit_solution(13822650039323046106)
XLA Ops:
  0.0 49.3 %shard_map.91 = f32[2,64]{1,0:T(2,128)} custom-call(bf16[128,2048]{1,0:T(8,128)(2,1)} %tokens.1, bf16[192,2048]{1,0:T(8,128)(2,1)} %bitcast.12, bf16[192,2048]{1,0:T(8,128)(2,1)} %bitcast.13, bf16[192,2048]{1,0:T(8,128)(2,1)} %bitcast.14, bf16[2048,128]{1,0:T(8,128)(2,1)} %proj.1, bf16[1024,128]{1,0:T(8,128)(2,1)} %bitcast.15, s32[4,128]{1,0:T(4,128)} %bitcast.16, ...), custom_call_target="tpu_custom_call" | custom-call | tf_op jit(solution)/shard_map/pallas_call | solution.py:448
  49.3 1.2 %copy.11 = f32[2,64]{1,0:T(2,128)} copy(f32[2,64]{1,0:T(2,128)} %shard_map.91) | data formatting | bytes 1024
